TPU v7x, 128 devices: a whole 4x4x4 slice. The times are simulated.
128 devices in a mesh: pipe: 8 (over y, x_lo), seq: 16 (over z, x_hi, core).
Axes of the slice: x: 4 (x_hi: 2, x_lo: 2; x = x_hi * 2 + x_lo), y: 4, z: 4, core: 2. Of those that a mesh axis runs over, the one named last changes fastest.
Arguments:
- held: bfloat16 [8, 2048, 1536], P('pipe', 'seq'), may hold values from -6 to 6
- entering: bfloat16 [2048, 1536], P('seq'), may hold values from -6 to 6
- counts: int32 [9], replicated, may hold values from 1 to 256
- kind: int32 [8], P('pipe'), may hold values from 0 to 1
- modulation: float32 [8, 6, 1536], P('pipe'), may hold values from -4 to 4
- w_qkv: bfloat16 [8, 1536, 6144], P('pipe'), may hold values from -0.15625 to 0.15625
- w_out: bfloat16 [8, 2048, 1536], P('pipe'), may hold values from -0.125 to 0.125
- q_gain: float32 [8, 128], P('pipe'), may hold values from 1.5 to 6
- k_gain: float32 [8, 128], P('pipe'), may hold values from 1.5 to 6
Outputs:
- arrived: bfloat16 [2, 8, 2048, 1536], P(None, 'pipe', 'seq')
All inputs are finite; a program needn't handle non-finite values.
Results may differ from a plain program's by a relative error of at most 0.023.
The roundings to bfloat16 on the way count: a program that leaves them out, or rounds other values in their place, can miss the bound.
Values may be sent and summed in bfloat16 or wider, within the bound.
A program may use at most 128 MiB of HBM per device.

v0:
```python
import jax
import jax.numpy as jnp
from jax import lax
from jax.sharding import PartitionSpec as P

HD = 128
TXT = 256


eps = 1e-06


def from_behind(value, axis, steps):
    count = lax.axis_size(axis)
    pairs = [(source, (source + steps) % count) for source in range(count)]
    return lax.ppermute(value, axis, pairs)


def rms_heads(values_f32, gain):
    return (
        values_f32
        * lax.rsqrt(jnp.mean(values_f32 * values_f32, axis=-1, keepdims=True) + eps)
        * gain
    )


def shards(held, entering, counts, kind, modulation, w_qkv, w_out, q_gain, k_gain):
    section_id = lax.axis_index("pipe")
    seq_rank = lax.axis_index("seq")
    seq_devices = lax.axis_size("seq")
    tok_rows = held.shape[1]
    seq_total = tok_rows * seq_devices
    text_start = seq_total - TXT
    inner_width = w_out.shape[1]
    head_count = inner_width // HD
    section_count = counts.shape[0] - 1
    positions = seq_rank * tok_rows + jnp.arange(tok_rows, dtype=jnp.int32)
    params = modulation[0]
    choose = ((positions >= text_start) & (kind[0] == 0))[:, None]
    shift_row = jnp.where(choose, params[3], params[0])
    scale_row = jnp.where(choose, params[4], params[1])
    gate_row = jnp.where(choose, params[5], params[2])
    factor_scale = HD ** (-0.5)

    def pass_on(outcome):
        return from_behind(outcome, "pipe", 1)

    def run_block(resid, text_live):
        resid_f32 = resid.astype(jnp.float32)
        center = resid_f32 - jnp.mean(resid_f32, axis=-1, keepdims=True)
        normed = center * lax.rsqrt(jnp.mean(center * center, axis=-1, keepdims=True) + eps)
        mixed_in = (normed * (1.0 + scale_row) + shift_row).astype(jnp.bfloat16)
        projected = jnp.dot(mixed_in, w_qkv[0], preferred_element_type=jnp.float32)
        query_heads = rms_heads(
            projected[:, :inner_width].reshape(tok_rows, head_count, HD), q_gain[0]
        ).astype(jnp.bfloat16)
        key_heads = rms_heads(
            projected[:, inner_width : 2 * inner_width].reshape(tok_rows, head_count, HD), k_gain[0]
        ).astype(jnp.bfloat16)
        value_heads = (
            projected[:, 2 * inner_width :].reshape(tok_rows, head_count, HD).astype(jnp.bfloat16)
        )
        key_limit = text_start + text_live
        row_top = jnp.full((head_count, tok_rows), -1e30, jnp.float32)
        key_piece = lax.all_gather(key_heads, "seq", axis=0, tiled=True)
        value_piece = lax.all_gather(value_heads, "seq", axis=0, tiled=True)
        scores = (
            jnp.einsum("qhd,khd->hqk", query_heads, key_piece, preferred_element_type=jnp.float32)
            * factor_scale
        )
        key_pos = jnp.arange(key_piece.shape[0], dtype=jnp.int32)
        scores = jnp.where((key_pos < key_limit)[None, None, :], scores, -1e30)
        new_top = jnp.maximum(row_top, jnp.max(scores, axis=-1))
        weights = jnp.exp(scores - new_top[..., None])
        denom = jnp.sum(weights, axis=-1)
        accum = jnp.einsum(
            "hqk,khd->hqd",
            weights.astype(jnp.bfloat16),
            value_piece,
            preferred_element_type=jnp.float32,
        )
        row_top, denom, accum = (new_top, denom, accum)
        attended = (accum / denom[..., None]).astype(jnp.bfloat16).transpose(1, 0, 2)
        merged = attended.reshape(tok_rows, inner_width)
        update = jnp.dot(merged, w_out[0], preferred_element_type=jnp.float32)
        return (resid_f32 + gate_row * update).astype(jnp.bfloat16)

    outcome_one = run_block(held[0], counts[section_id])
    arrived_one = pass_on(outcome_one)
    inputs_two = jnp.where(section_id == 0, entering, arrived_one)
    outcome_two = run_block(inputs_two, counts[(section_id + section_count) % (section_count + 1)])
    arrived_two = pass_on(outcome_two)
    return jnp.stack([arrived_one, arrived_two])[:, None]


def solution(mesh):
    placed = (
        P("pipe", "seq", None),
        P("seq", None),
        P(),
        P("pipe"),
        P("pipe", None, None),
        P("pipe", None, None),
        P("pipe", None, None),
        P("pipe", None),
        P("pipe", None),
    )
    return jax.shard_map(
        shards, mesh=mesh, in_specs=placed, out_specs=P(None, "pipe", "seq", None), check_vma=False
    )
```

profile of v0, /device:TPU:1, one launch (start us, length us, event | category | flops | bytes accessed | tf_op | source)
XLA Modules:
  0.0 398.3 jit_solution(795105245037220855)
XLA Ops:
  10.6 8.1 %fusion.2 = f32[128,6144]{1,0:T(8,128)S(1)} fusion(bf16[1,1536,6144]{2,1,0:T(8,128)(2,1)} %param.14, bf16[1,128,1536]{2,1,0:T(8,128)(2,1)} %param.9, f32[1536]{0:T(1024)S(1)} %get-tuple-element.9, f32[1536]{0:T(1024)S(1)} %get-tuple-element.10, f32[1536]{0:T(1024)S(1)} %get-tuple-element.6, f32[1536]{0:T(1024)S(1)} %get-tuple-element.7, ...), kind=kOutput, calls=%fused_computation.2 | convolution fusion | flops 2417688576 | bytes 22439040 | tf_op jit(solution)/shard_map/dot_general | solution.py:53
  18.7 1.6 slice_bitcast_fusion.1
  21.0 2.4 fusion.51
  24.3 2.0 copy.58
  26.4 1.4 copy.61
  30.0 70.0 %all-gather.5.cloned.1.call-done = bf16[2048,16,128]{2,0,1:T(8,128)(2,1)} async-done(((bf16[128,16,128]{2,0,1:T(8,128)(2,1)}), bf16[2048,16,128]{2,0,1:T(8,128)(2,1)}) %all-gather.5.cloned.1.call-update) | async-done | bytes 8388624 | tf_op jit(solution)/shard_map/all_gather | solution.py:65
  100.0 12.1 %fusion.4 = (f32[16,128]{1,0:T(8,128)S(1)}, f32[16,128,2048]{2,1,0:T(8,128)}) fusion(pred[2048]{0:T(1024)(128)(4,1)S(1)} %iota_compare_fusion.1, bf16[2048,16,128]{2,0,1:T(8,128)(2,1)} %all-gather.5.cloned.1.call-done, bf16[128,16,128]{2,1,0:T(8,128)(2,1)S(1)} %multiply_convert_fusion.2), kind=kOutput, calls=%fused_computation.8 | convolution fusion | flops 1086322688 | bytes 25700352 | tf_op jit(solution)/shard_map/qhd,khd->hqk/dot_general | solution.py:68
  112.1 7.9 %fusion.6 = f32[16,128]{1,0:T(8,128)S(1)} fusion(f32[16,128,2048]{2,1,0:T(8,128)} %get-tuple-element.21, f32[16,128]{1,0:T(8,128)S(1)} %broadcast_maximum_fusion.1, pred[2048]{0:T(1024)(128)(4,1)S(1)} %iota_compare_fusion.1), kind=kLoop, calls=%fused_computation.10 | loop fusion | flops 16775168 | bytes 16795648 | tf_op jit(solution)/shard_map/reduce_sum | solution.py:75
  120.0 56.6 %all-gather.7.cloned.1.call-done = bf16[2048,16,128]{0,2,1:T(8,128)(2,1)} async-done(((bf16[128,16,128]{0,2,1:T(8,128)(2,1)}), bf16[2048,16,128]{0,2,1:T(8,128)(2,1)}) %all-gather.7.cloned.1.call-update) | async-done | bytes 8388624 | tf_op jit(solution)/shard_map/all_gather | solution.py:66
  176.6 10.7 %divide_convert_fusion.1 = bf16[128,16,128]{0,2,1:T(8,128)(2,1)S(1)} fusion(bf16[2048,16,128]{0,2,1:T(8,128)(2,1)} %all-gather.7.cloned.1.call-done, f32[16,128,2048]{2,1,0:T(8,128)} %get-tuple-element.21, f32[16,128]{1,0:T(8,128)S(1)} %broadcast_maximum_fusion.1, pred[2048]{0:T(1024)(128)(4,1)S(1)} %iota_compare_fusion.1, f32[128,16]{0,1:T(8,128)S(1)} %bitcast.101), kind=kOutput, calls=%fused_computation.53 | convolution fusion | flops 1091043328 | bytes 25708544 | tf_op jit(solution)/shard_map/hqk,khd->hqd/dot_general | solution.py:76
  189.0 12.2 %collective-permute-done = bf16[128,1536]{1,0:T(8,128)(2,1)S(1)} collective-permute-done((bf16[128,1536]{1,0:T(8,128)(2,1)S(1)}, bf16[128,1536]{1,0:T(8,128)(2,1)S(1)}, u32[]{:S(2)}, u32[]{:S(2)}) %collective-permute-start) | collective-permute-done | bytes 393248 | tf_op jit(solution)/shard_map/ppermute | solution.py:16
  202.0 8.1 %fusion = f32[128,6144]{1,0:T(8,128)S(1)} fusion(bf16[1,1536,6144]{2,1,0:T(8,128)(2,1)} %param.14, bf16[128,1536]{1,0:T(8,128)(2,1)S(1)} %get-tuple-element.12, f32[1536]{0:T(1024)} %copy-done.4, f32[1536]{0:T(1024)} %copy-done.5, f32[1536]{0:T(1024)S(1)} %get-tuple-element.6, f32[1536]{0:T(1024)S(1)} %get-tuple-element.7, f32[128]{0:T(128)S(1)} %add_rsqrt_fusion.4, ...), kind=kOutput, calls=%fused_computation | convolution fusion | flops 2417688576 | bytes 22439040 | tf_op jit(solution)/shard_map/dot_general | solution.py:53
  210.1 1.5 slice_bitcast_fusion
  211.6 2.5 copy.53
  215.4 2.6 copy.54
  218.0 2.4 multiply_convert_fusion
  221.3 2.0 copy.59
  224.0 1.4 copy.63
  226.3 63.6 %all-gather.9.cloned.1.call-done = bf16[2048,16,128]{2,0,1:T(8,128)(2,1)} async-done(((bf16[128,16,128]{2,0,1:T(8,128)(2,1)}), bf16[2048,16,128]{2,0,1:T(8,128)(2,1)}) %all-gather.9.cloned.1.call-update) | async-done | bytes 8388624 | tf_op jit(solution)/shard_map/all_gather | solution.py:65
  289.9 12.1 %fusion.5 = (f32[16,128]{1,0:T(8,128)S(1)}, f32[16,128,2048]{2,1,0:T(8,128)}) fusion(pred[2048]{0:T(1024)(128)(4,1)S(1)} %iota_compare_fusion, bf16[2048,16,128]{2,0,1:T(8,128)(2,1)} %all-gather.9.cloned.1.call-done, bf16[128,16,128]{2,1,0:T(8,128)(2,1)S(1)} %multiply_convert_fusion.1), kind=kOutput, calls=%fused_computation.9 | convolution fusion | flops 1086322688 | bytes 25700352 | tf_op jit(solution)/shard_map/qhd,khd->hqk/dot_general | solution.py:68
  302.0 7.9 %fusion.8 = f32[16,128]{1,0:T(8,128)S(1)} fusion(f32[16,128,2048]{2,1,0:T(8,128)} %get-tuple-element.23, f32[16,128]{1,0:T(8,128)S(1)} %broadcast_maximum_fusion, pred[2048]{0:T(1024)(128)(4,1)S(1)} %iota_compare_fusion), kind=kLoop, calls=%fused_computation.12 | loop fusion | flops 16775168 | bytes 16795648 | tf_op jit(solution)/shard_map/reduce_sum | solution.py:75
  309.9 56.4 %all-gather.11.cloned.1.call-done = bf16[2048,16,128]{0,2,1:T(8,128)(2,1)} async-done(((bf16[128,16,128]{0,2,1:T(8,128)(2,1)}), bf16[2048,16,128]{0,2,1:T(8,128)(2,1)}) %all-gather.11.cloned.1.call-update) | async-done | bytes 8388624 | tf_op jit(solution)/shard_map/all_gather | solution.py:66
  366.4 10.7 %divide_convert_fusion = bf16[128,16,128]{0,2,1:T(8,128)(2,1)S(1)} fusion(bf16[2048,16,128]{0,2,1:T(8,128)(2,1)} %all-gather.11.cloned.1.call-done, f32[16,128,2048]{2,1,0:T(8,128)} %get-tuple-element.23, f32[16,128]{1,0:T(8,128)S(1)} %broadcast_maximum_fusion, pred[2048]{0:T(1024)(128)(4,1)S(1)} %iota_compare_fusion, f32[128,16]{0,1:T(8,128)S(1)} %bitcast.102), kind=kOutput, calls=%fused_computation.48 | convolution fusion | flops 1091043328 | bytes 25708544 | tf_op jit(solution)/shard_map/hqk,khd->hqd/dot_general | solution.py:76
  378.6 12.2 %collective-permute-done.1 = bf16[128,1536]{1,0:T(8,128)(2,1)S(1)} collective-permute-done((bf16[128,1536]{1,0:T(8,128)(2,1)S(1)}, bf16[128,1536]{1,0:T(8,128)(2,1)S(1)}, u32[]{:S(2)}, u32[]{:S(2)}) %collective-permute-start.1) | collective-permute-done | bytes 393248 | tf_op jit(solution)/shard_map/ppermute | solution.py:16
  (88 shorter events, 14.2 us)
Async XLA Ops:
  6.5 93.4 %all-gather.5.cloned.1.call-start = ((), (), s32[]{:S(2)}) async-start(), calls=%async_computation | async-start | bytes 8912896 | tf_op jit(solution)/shard_map/all_gather | solution.py:65
  7.4 13.1 %copy-start.4 = (f32[1536]{0:T(1024)}, f32[1536]{0:T(1024)S(1)}, u32[]{:S(2)}) copy-start(f32[1536]{0:T(1024)S(1)} %get-tuple-element.9) | copy-start | bytes 18436
  7.4 13.1 %copy-start.5 = (f32[1536]{0:T(1024)}, f32[1536]{0:T(1024)S(1)}, u32[]{:S(2)}) copy-start(f32[1536]{0:T(1024)S(1)} %get-tuple-element.10) | copy-start | bytes 18436
  7.4 179.9 %copy-start.6 = (f32[1536]{0:T(1024)}, f32[1536]{0:T(1024)S(1)}, u32[]{:S(2)}) copy-start(f32[1536]{0:T(1024)S(1)} %get-tuple-element.5) | copy-start | bytes 18436
  7.4 179.9 %copy-start.8 = (f32[1536]{0:T(1024)}, f32[1536]{0:T(1024)S(1)}, u32[]{:S(2)}) copy-start(f32[1536]{0:T(1024)S(1)} %get-tuple-element.8) | copy-start | bytes 18436
  10.5 176.8 %copy-start.10 = (pred[128]{0:T(512)(128)(4,1)}, pred[128]{0:T(512)(128)(4,1)S(1)}, u32[]{:S(2)}) copy-start(pred[128]{0:T(512)(128)(4,1)S(1)} %compare_and_fusion) | copy-start | bytes 388
  10.5 17.9 %copy-start.15 = (s32[9]{0:T(128)S(1)}, s32[9]{0:T(128)}, u32[]{:S(2)}) copy-start(s32[9]{0:T(128)} %param.11) | copy-start | bytes 112
  10.6 19.1 %copy-start.13 = (f32[1,128]{1,0:T(1,128)S(1)}, f32[1,128]{1,0:T(1,128)}, u32[]{:S(2)}) copy-start(f32[1,128]{1,0:T(1,128)} %param.16) | copy-start | bytes 1540
  23.4 153.2 %all-gather.7.cloned.1.call-start = ((), (), s32[]{:S(2)}) async-start(), calls=%async_computation.1 | async-start | bytes 8912896 | tf_op jit(solution)/shard_map/all_gather | solution.py:66
  26.4 263.5 %all-gather.9.cloned.1.call-start = ((), (), s32[]{:S(2)}) async-start(), calls=%async_computation.2 | async-start | bytes 8912896 | tf_op jit(solution)/shard_map/all_gather | solution.py:65
  112.1 75.3 %slice-start = ((s8[6291456]{0:T(1024)(128)(4,1)}), s8[2097152]{0:T(1024)(128)(4,1)S(1)}, s32[]{:S(2)}) async-start(s8[6291456]{0:T(1024)(128)(4,1)} %bitcast.87), calls=%async_computation.4 | async-start | bytes 4194304
  176.6 10.8 %slice-start.1 = ((s8[6291456]{0:T(1024)(128)(4,1)}), s8[4194304]{0:T(1024)(128)(4,1)S(1)}, s32[]{:S(2)}) async-start(s8[6291456]{0:T(1024)(128)(4,1)} %bitcast.87), calls=%async_computation.5 | async-start | bytes 8388608
  176.6 10.8 %copy-start = (bf16[1,128,1536]{2,1,0:T(8,128)(2,1)S(1)}, bf16[1,128,1536]{2,1,0:T(8,128)(2,1)}, u32[]{:S(2)}) copy-start(bf16[1,128,1536]{2,1,0:T(8,128)(2,1)} %param.9) | copy-start | bytes 1179652
  176.6 24.6 %copy-start.3 = (bf16[128,1536]{1,0:T(8,128)(2,1)S(1)}, bf16[128,1536]{1,0:T(8,128)(2,1)}, u32[]{:S(2)}) copy-start(bf16[128,1536]{1,0:T(8,128)(2,1)} %param.10) | copy-start | bytes 1179652
  188.5 12.8 %collective-permute-start = (bf16[128,1536]{1,0:T(8,128)(2,1)S(1)}, bf16[128,1536]{1,0:T(8,128)(2,1)S(1)}, u32[]{:S(2)}, u32[]{:S(2)}) collective-permute-start(bf16[128,1536]{1,0:T(8,128)(2,1)S(1)} %fusion.41), channel_id=1, source_target_pairs={{0,16},{16,32},{32,48},{48,64},{64,80},{80,96},{96,112},{112,0},{1... | collective-permute-start | bytes 1179656 | tf_op jit(solution)/shard_map/ppermute | solution.py:16
  210.0 15.9 %copy-start.14 = (f32[1,128]{1,0:T(1,128)S(1)}, f32[1,128]{1,0:T(1,128)}, u32[]{:S(2)}) copy-start(f32[1,128]{1,0:T(1,128)} %param.16) | copy-start | bytes 1540
  220.4 145.9 %all-gather.11.cloned.1.call-start = ((), (), s32[]{:S(2)}) async-start(), calls=%async_computation.3 | async-start | bytes 8912896 | tf_op jit(solution)/shard_map/all_gather | solution.py:66
  302.0 75.1 %slice-start.2 = ((s8[6291456]{0:T(1024)(128)(4,1)}), s8[2097152]{0:T(1024)(128)(4,1)S(1)}, s32[]{:S(2)}) async-start(s8[6291456]{0:T(1024)(128)(4,1)} %bitcast.89), calls=%async_computation.6 | async-start | bytes 4194304
  366.3 10.8 %slice-start.3 = ((s8[6291456]{0:T(1024)(128)(4,1)}), s8[4194304]{0:T(1024)(128)(4,1)S(1)}, s32[]{:S(2)}) async-start(s8[6291456]{0:T(1024)(128)(4,1)} %bitcast.89), calls=%async_computation.7 | async-start | bytes 8388608
  366.3 10.8 %copy-start.7 = (f32[1536]{0:T(1024)S(1)}, f32[1536]{0:T(1024)}, u32[]{:S(2)}) copy-start(f32[1536]{0:T(1024)} %copy-done.6) | copy-start | bytes 18436
  366.3 10.8 %copy-start.9 = (f32[1536]{0:T(1024)S(1)}, f32[1536]{0:T(1024)}, u32[]{:S(2)}) copy-start(f32[1536]{0:T(1024)} %copy-done.8) | copy-start | bytes 18436
  366.3 10.8 %copy-start.11 = (pred[128]{0:T(512)(128)(4,1)S(1)}, pred[128]{0:T(512)(128)(4,1)}, u32[]{:S(2)}) copy-start(pred[128]{0:T(512)(128)(4,1)} %copy-done.10) | copy-start | bytes 388
  366.4 24.4 %copy-start.2 = (bf16[128,1536]{1,0:T(8,128)(2,1)S(1)}, bf16[128,1536]{1,0:T(8,128)(2,1)}, u32[]{:S(2)}) copy-start(bf16[128,1536]{1,0:T(8,128)(2,1)} %copy-done.1) | copy-start | bytes 1179652
  378.2 12.6 %collective-permute-start.1 = (bf16[128,1536]{1,0:T(8,128)(2,1)S(1)}, bf16[128,1536]{1,0:T(8,128)(2,1)S(1)}, u32[]{:S(2)}, u32[]{:S(2)}) collective-permute-start(bf16[128,1536]{1,0:T(8,128)(2,1)S(1)} %fusion.38), channel_id=1, source_target_pairs={{0,16},{16,32},{32,48},{48,64},{64,80},{80,96},{96,112},{112,0},{1... | collective-permute-start | bytes 1179656 | tf_op jit(solution)/shard_map/ppermute | solution.py:16
  (2 other events, 11.2 us)
Sparse Core Ops, SparseCore 0:
  23.5 76.4 all-gather.4
  102.3 74.2 all-gather.6
  220.5 69.2 all-gather.8
  292.1 74.2 all-gather.10
where the time goes:
time: 399 us; the launch traced here: 398 us
  waiting for transfers between devices  271 us (68%)
  matrix products  64 us (16%)
  other arithmetic  27.4 us (7%)
  local copies, waits for them, and re-layouts  19.3 us (5%)
  between operations  15.4 us (4%)
    all_gather x2, waiting for transfers between devices, run_block(): key_piece = lax.all_gather(key_heads, 'seq', axis=0, tiled=True)  134 us
    all_gather x2, waiting for transfers between devices, run_block(): value_piece = lax.all_gather(value_heads, 'seq', axis=0, tiled=True)  113 us
    ppermute x2, waiting for transfers between devices, from_behind(): return lax.ppermute(value, axis, pairs)  24.5 us
    dot_general x2, matrix products, run_block(): jnp.einsum('qhd,khd->hqk', query_heads, key_piece, preferred_element_type...  24.3 us
    dot_general x2, matrix products, run_block(): jnp.einsum('hqk,khd->hqd', weights.astype(jnp.bfloat16), value_piece, pre...  21.5 us
    dot_general x2, matrix products, run_block(): projected = jnp.dot(mixed_in, w_qkv[0], preferred_element_type=jnp.float32)  16.2 us
    reduce_sum x2, other arithmetic, run_block(): denom = jnp.sum(weights, axis=-1)  15.8 us
  transfers between devices with their start and end apart: 6, of which 6 were waited for; matrix products, arithmetic and copies ran while one was open for 13% of the time, Pallas kernels for 0%

commit v1 on v0

v1 whole, which is shorter than its diff:
```python
import functools

import jax
import jax.numpy as jnp
from jax import lax
from jax.experimental import pallas as pl
from jax.experimental.pallas import tpu as pltpu
from jax.sharding import PartitionSpec as P

HD = 128
TXT = 256
EPS = 1e-06
MESH = pl.DeviceIdType.MESH
LOG2E = 1.4426950408889634

HOPS = (2, 1, 3, 0)


def body(
    counts_ref,
    kind_ref,
    held_hbm,
    entering_hbm,
    mod_ref,
    wqkv_hbm,
    wout_hbm,
    qg_ref,
    kg_ref,
    out_ref,
    w_ref,
    wo_ref,
    xin_ref,
    xother_ref,
    xsend_ref,
    mixed_ref,
    qkv_ref,
    qkvs_ref,
    att_ref,
    atts_ref,
    load_sem,
    w_sem,
    wo_sem,
    cross_send,
    cross_recv,
    qkv_send,
    qkv_recv,
    att_send,
    att_recv,
    pipe_send,
    pipe_recv,
):
    rows, width = xin_ref.shape[1], xin_ref.shape[2]
    inner = wo_ref.shape[0]
    section = lax.axis_index("pipe")
    rank = lax.axis_index("seq")
    sections = lax.axis_size("pipe")
    ranks = lax.axis_size("seq")
    z, xh, core = rank // 4, (rank // 2) % 2, rank % 2
    other = z * 4 + (1 - xh) * 2 + core
    following = (section + 1) % sections
    before = (section + sections - 1) % sections
    seq_total = rows * ranks
    text_start = seq_total - TXT

    barrier = pltpu.get_barrier_semaphore()
    for step in range(1, ranks):
        pl.semaphore_signal(
            barrier, 1, device_id=(section, (rank + step) % ranks), device_id_type=MESH
        )
    for there in (following, before):
        for column in (rank, other):
            pl.semaphore_signal(barrier, 1, device_id=(there, column), device_id_type=MESH)

    loads = [
        pltpu.make_async_copy(held_hbm.at[0], xin_ref.at[0], load_sem.at[0]),
        pltpu.make_async_copy(entering_hbm, xin_ref.at[1], load_sem.at[1]),
    ]
    for copy in loads:
        copy.start()
    weight_loads = []
    for j, hop in enumerate(HOPS):
        for cc in range(2):
            head = ((z + hop) % 4) * 4 + xh * 2 + (core + cc) % 2
            for part in range(3):
                copy = pltpu.make_async_copy(
                    wqkv_hbm.at[
                        0, :, pl.ds(pl.multiple_of(part * inner + head * HD, HD), HD)
                    ],
                    w_ref.at[j, :, pl.ds((part * 2 + cc) * HD, HD)],
                    w_sem.at[j, cc, part],
                )
                copy.start()
                weight_loads.append(copy)
    wo_load = pltpu.make_async_copy(wout_hbm.at[0], wo_ref, wo_sem)
    wo_load.start()

    for copy in loads:
        copy.wait()
    pl.semaphore_wait(barrier, ranks - 1 + 4)

    cross_one = pltpu.make_async_remote_copy(
        xin_ref.at[0],
        xother_ref.at[0],
        cross_send.at[0],
        cross_recv.at[0],
        device_id=(section, other),
        device_id_type=MESH,
    )
    cross_one.start()
    cross_two = pltpu.make_async_remote_copy(
        xin_ref.at[1],
        xother_ref.at[1],
        cross_send.at[1],
        cross_recv.at[1],
        device_id=(section, other),
        device_id_type=MESH,
    )

    @pl.when(section == 0)
    def _():
        cross_two.start()

    kind_row = jnp.full((1, width), kind_ref[0], jnp.int32)

    def mod_row(index, column):
        text = (column >= text_start // rows).astype(jnp.int32)
        pick = (kind_row == 0) & (jnp.full((1, width), text, jnp.int32) == 1)
        return jnp.where(pick, mod_ref[0, index + 3 : index + 4], mod_ref[0, index : index + 1])

    def mix(x, half, column):
        x = x.astype(jnp.float32)
        center = x - jnp.mean(x, axis=-1, keepdims=True)
        normed = center * lax.rsqrt(jnp.mean(center * center, axis=-1, keepdims=True) + EPS)
        mixed = normed * (1.0 + mod_row(1, column)) + mod_row(0, column)
        mixed_ref[half] = mixed.astype(jnp.bfloat16)

    def qkv_copy(step, half, j, cc, column):
        target = ((z + HOPS[j]) % 4) * 4 + xh * 2 + (core + cc) % 2
        return pltpu.make_async_remote_copy(
            qkvs_ref.at[step, half, j, cc],
            qkv_ref.at[step, pl.ds(pl.multiple_of(column * rows, rows), rows), :],
            qkv_send.at[step, half, j, cc],
            qkv_recv.at[step, half, j, cc],
            device_id=(section, target),
            device_id_type=MESH,
        )

    def rms(values, gain):
        return (
            values
            * lax.rsqrt(jnp.mean(values * values, axis=-1, keepdims=True) + EPS)
            * gain
        ).astype(jnp.bfloat16)

    def project(step, half, column):
        for j, hop in enumerate(HOPS):
            if step == 0 and half == 0:
                for copy in weight_loads[j * 6 : (j + 1) * 6]:
                    copy.wait()
            product = jnp.dot(
                mixed_ref[half], w_ref[j], preferred_element_type=jnp.float32
            )
            for cc in range(2):
                query, key, value = (
                    product[:, (part * 2 + cc) * HD : (part * 2 + cc + 1) * HD]
                    for part in range(3)
                )
                query = rms(query, qg_ref[...])
                key = rms(key, kg_ref[...])
                value = value.astype(jnp.bfloat16)
                if hop == 0 and cc == 0:
                    slot = pl.ds(pl.multiple_of(column * rows, rows), rows)
                    qkv_ref[step, slot, 0:HD] = query
                    qkv_ref[step, slot, HD : 2 * HD] = key
                    qkv_ref[step, slot, 2 * HD : 3 * HD] = value
                else:
                    qkvs_ref[step, half, j, cc, :, 0:HD] = query
                    qkvs_ref[step, half, j, cc, :, HD : 2 * HD] = key
                    qkvs_ref[step, half, j, cc, :, 2 * HD : 3 * HD] = value
                    qkv_copy(step, half, j, cc, column).start()

    def remote_pairs():
        return [(j, cc) for j in range(4) for cc in range(2) if HOPS[j] or cc]

    def att_copy(step, i, cc):
        zt = (z + i + 1) % 4
        xt = (xh + 1 - i // 4) % 2
        ct = (core + cc) % 2
        return pltpu.make_async_remote_copy(
            atts_ref.at[step, i, pl.ds(pl.multiple_of(ct * rows, rows), rows), :],
            att_ref.at[step, :, pl.ds(pl.multiple_of(rank * HD, HD), HD)],
            att_send.at[step, i, cc],
            att_recv.at[step, i, cc],
            device_id=(section, zt * 4 + xt * 2 + ct),
            device_id_type=MESH,
        )

    def attend(step, live):
        limit = jnp.full((2 * rows, TXT), text_start + live, jnp.int32)

        def chunk(i, carry):
            zt = (z + i + 1) % 4
            xt = (xh + 1 - i // 4) % 2
            start = pl.multiple_of((zt * 4 + xt * 2) * rows, 2 * rows)
            query = qkv_ref[step, pl.ds(start, 2 * rows), 0:HD]
            scores = lax.dot_general(
                query,
                qkv_ref[step, :, HD : 2 * HD],
                (((1,), (1,)), ((), ())),
                preferred_element_type=jnp.float32,
            )
            place = text_start + lax.broadcasted_iota(jnp.int32, (2 * rows, TXT), 1)
            tail = jnp.where(place < limit, scores[:, text_start:], -1e30)
            scores = jnp.concatenate([scores[:, :text_start], tail], axis=1)
            top = jnp.max(scores, axis=-1, keepdims=True)
            weights = jnp.exp2((scores - top) * (HD ** (-0.5) * LOG2E))
            denom = jnp.sum(weights, axis=-1, keepdims=True)
            summed = jnp.dot(
                weights.astype(jnp.bfloat16),
                qkv_ref[step, :, 2 * HD : 3 * HD],
                preferred_element_type=jnp.float32,
            )
            atts_ref[step, i] = (summed / denom).astype(jnp.bfloat16)

            @pl.when(i < 7)
            def _():
                att_copy(step, i, 0).start()

            att_copy(step, i, 1).start()
            return carry

        lax.fori_loop(0, 8, chunk, 0)
        att_ref[step, :, pl.ds(pl.multiple_of(rank * HD, HD), HD)] = atts_ref[
            step, 7, pl.ds(pl.multiple_of(core * rows, rows), rows), :
        ]

    def finish(step, x):
        gate = mod_row(2, rank)
        tile = 512
        for n in range(width // tile):
            cols = slice(n * tile, (n + 1) * tile)
            update = jnp.dot(
                att_ref[step], wo_ref[:, cols], preferred_element_type=jnp.float32
            )
            xsend_ref[step, :, cols] = (
                x[:, cols].astype(jnp.float32) + gate[:, cols] * update
            ).astype(jnp.bfloat16)

    def pipe_copy(step, column, which):
        return pltpu.make_async_remote_copy(
            xsend_ref.at[step],
            out_ref.at[step] if which == 0 else xother_ref.at[1],
            pipe_send.at[step, which],
            pipe_recv.at[step] if which == 0 else cross_recv.at[1],
            device_id=(following, column),
            device_id_type=MESH,
        )

    mix(xin_ref[0], 0, rank)
    project(0, 0, rank)
    cross_one.wait()
    mix(xother_ref[0], 1, other)
    project(0, 1, other)

    def middle(step, live):
        for half, column in ((0, rank), (1, other)):
            for j, cc in remote_pairs():
                qkv_copy(step, half, j, cc, column).wait_recv()
        attend(step, live)
        for i in range(8):
            for cc in range(2):
                if i < 7 or cc:
                    att_copy(step, i, cc).wait_recv()

    middle(0, counts_ref[section])
    wo_load.wait()
    finish(0, xin_ref[0])
    pipe_copy(0, rank, 0).start()

    @pl.when(section < sections - 1)
    def _():
        pipe_copy(0, other, 1).start()

    pipe_copy(0, rank, 0).wait_recv()

    @pl.when(section > 0)
    def _():
        xin_ref[1] = out_ref[0]

    mix(xin_ref[1], 0, rank)
    project(1, 0, rank)
    cross_two.wait_recv()
    mix(xother_ref[1], 1, other)
    project(1, 1, other)
    middle(1, counts_ref[(section + sections) % (sections + 1)])
    finish(1, xin_ref[1])
    pipe_copy(1, rank, 0).start()

    @pl.when(section == 0)
    def _():
        cross_two.wait_send()

    @pl.when(section < sections - 1)
    def _():
        pipe_copy(0, other, 1).wait_send()

    pipe_copy(0, rank, 0).wait_send()
    for step in range(2):
        for half, column in ((0, rank), (1, other)):
            for j, cc in remote_pairs():
                qkv_copy(step, half, j, cc, column).wait_send()
        for i in range(8):
            for cc in range(2):
                if i < 7 or cc:
                    att_copy(step, i, cc).wait_send()
    pipe_copy(1, rank, 0).wait()


def shards(held, entering, counts, kind, modulation, w_qkv, w_out, q_gain, k_gain):
    rows, width = entering.shape
    inner = w_out.shape[1]
    ranks = lax.axis_size("seq")
    bf16 = jnp.bfloat16
    vmem = pl.BlockSpec(memory_space=pltpu.VMEM)
    smem = pl.BlockSpec(memory_space=pltpu.SMEM)
    hbm = pl.BlockSpec(memory_space=pl.ANY)
    dma = pltpu.SemaphoreType.DMA
    out = pl.pallas_call(
        body,
        out_shape=jax.ShapeDtypeStruct((2, rows, width), bf16),
        in_specs=[smem, smem, hbm, hbm, vmem, hbm, hbm, vmem, vmem],
        out_specs=vmem,
        scratch_shapes=[
            pltpu.VMEM((4, width, 6 * HD), bf16),
            pltpu.VMEM((inner, width), bf16),
            pltpu.VMEM((2, rows, width), bf16),
            pltpu.VMEM((2, rows, width), bf16),
            pltpu.VMEM((2, rows, width), bf16),
            pltpu.VMEM((2, rows, width), bf16),
            pltpu.VMEM((2, rows * ranks, 3 * HD), bf16),
            pltpu.VMEM((2, 2, 4, 2, rows, 3 * HD), bf16),
            pltpu.VMEM((2, rows, inner), bf16),
            pltpu.VMEM((2, 8, 2 * rows, HD), bf16),
            dma((2,)),
            dma((4, 2, 3)),
            dma,
            dma((2,)),
            dma((2,)),
            dma((2, 2, 4, 2)),
            dma((2, 2, 4, 2)),
            dma((2, 8, 2)),
            dma((2, 8, 2)),
            dma((2, 2)),
            dma((2,)),
        ],
        compiler_params=pltpu.CompilerParams(
            collective_id=0, has_side_effects=True, vmem_limit_bytes=60 * 1024 * 1024
        ),
        name="relay",
    )(counts, kind, held, entering, modulation, w_qkv, w_out, q_gain, k_gain)
    return out[:, None]


def solution(mesh):
    placed = (
        P("pipe", "seq", None),
        P("seq", None),
        P(),
        P("pipe"),
        P("pipe", None, None),
        P("pipe", None, None),
        P("pipe", None, None),
        P("pipe", None),
        P("pipe", None),
    )
    return jax.shard_map(
        shards, mesh=mesh, in_specs=placed, out_specs=P(None, "pipe", "seq", None), check_vma=False
    )
```

time: 399 us -> 110 us (0.28)
  the two profiles are of different devices: /device:TPU:1 before, /device:TPU:26 now
where the time goes in v1:
time: 110 us
  Pallas kernels  105 us (95%)
  local copies, waits for them, and re-layouts  3.46 us (3%)
    pallas_call x1, Pallas kernels, shards(): pl.pallas_call(body, out_shape=jax.ShapeDtypeStruct((2, rows, width), bf1...  105 us
    unnamed x2, local copies, waits for them, and re-layouts  3.46 us

profile of v1, /device:TPU:26, one launch (start us, length us, event | category | flops | bytes accessed | tf_op | source)
XLA Modules:
  0.0 109.6 jit_solution(14595313108084642187)
XLA Ops:
  0.7 1.4 %copy.10.mod_ref = f32[1,6,1536]{2,1,0:T(8,128)} copy(f32[1,6,1536]{2,0,1:T(1,128)} %param.13) | data formatting | bytes 73728 | tf_op args[4]
  2.0 105.5 %relay.1 = bf16[2,128,1536]{2,1,0:T(8,128)(2,1)} custom-call(s32[9]{0:T(128)} %counts_ref.1, s32[1]{0:T(128)S(6)} %copy.13.kind_ref, bf16[1,128,1536]{2,1,0:T(8,128)(2,1)} %held_hbm.1, bf16[128,1536]{1,0:T(8,128)(2,1)} %entering_hbm.1, f32[1,6,1536]{2,1,0:T(8,128)} %copy.10.mod_ref, bf16[1,1536,6144]{2,1,0:T(8,128)(2,1)} %wqkv_hbm.1, ...), custom_call_target="tpu_custom_call" | custom-call | tf_op jit(solution)/shard_map/relay/pallas_call | solution.py:328
  107.5 2.1 %copy.14 = bf16[2,1,128,1536]{3,2,1,0:T(8,128)(2,1)} copy(bf16[2,1,128,1536]{3,2,1,0:T(8,128)(2,1)} %bitcast.3) | data formatting | bytes 1572864

commit v2 on v1

v2 whole, which is shorter than its diff:
```python
import functools

import jax
import jax.numpy as jnp
from jax import lax
from jax.experimental import pallas as pl
from jax.experimental.pallas import tpu as pltpu
from jax.sharding import PartitionSpec as P

HD = 128
TXT = 256
EPS = 1e-06
MESH = pl.DeviceIdType.MESH
LOG2E = 1.4426950408889634

HOPS = (2, 1, 3, 0)
PARTS = 4


def body(
    counts_ref,
    kind_ref,
    held_hbm,
    entering_hbm,
    mod_ref,
    wqkv_hbm,
    wout_hbm,
    qg_ref,
    kg_ref,
    out_ref,
    w_ref,
    wo_ref,
    xin_ref,
    xother_ref,
    xsend_ref,
    relay_ref,
    mixed_ref,
    kv_ref,
    q_ref,
    kvs_ref,
    qs_ref,
    att_ref,
    atts_ref,
    load_sem,
    w_sem,
    wo_sem,
    cross_send,
    cross_recv,
    kv_send,
    kv_recv,
    q_send,
    q_recv,
    att_send,
    att_recv,
    pipe_send,
    pipe_recv,
    relay_recv,
    relay_send,
):
    rows, width = xin_ref.shape[1], xin_ref.shape[2]
    half = rows // 2
    part = rows // PARTS
    inner = wo_ref.shape[0]
    section = lax.axis_index("pipe")
    rank = lax.axis_index("seq")
    sections = lax.axis_size("pipe")
    ranks = lax.axis_size("seq")
    z, xh, core = rank // 4, (rank // 2) % 2, rank % 2
    other = z * 4 + (1 - xh) * 2 + core
    place = z * 2 + core
    following = (section + 1) % sections
    before = (section + sections - 1) % sections
    ahead = (section + 2) % sections
    behind = (section + sections - 2) % sections
    odd = section % 2 == 1
    text_start = rows * ranks - TXT

    barrier = pltpu.get_barrier_semaphore()
    for step in range(1, ranks):
        pl.semaphore_signal(
            barrier, 1, device_id=(section, (rank + step) % ranks), device_id_type=MESH
        )
    for there in (following, before):
        for column in (rank, other):
            pl.semaphore_signal(barrier, 1, device_id=(there, column), device_id_type=MESH)
    for there in (ahead, behind):
        pl.semaphore_signal(barrier, 1, device_id=(there, rank), device_id_type=MESH)

    loads = [
        pltpu.make_async_copy(held_hbm.at[0], xin_ref.at[0], load_sem.at[0]),
        pltpu.make_async_copy(entering_hbm, xin_ref.at[1], load_sem.at[1]),
    ]
    for copy in loads:
        copy.start()
    weight_loads = {}
    for hop in HOPS:
        for cc in range(2):
            head = ((z + hop) % 4) * 4 + xh * 2 + (core + cc) % 2
            for third in range(3):
                copy = pltpu.make_async_copy(
                    wqkv_hbm.at[
                        0, :, pl.ds(pl.multiple_of(third * inner + head * HD, HD), HD)
                    ],
                    w_ref.at[hop, :, pl.ds((third * 2 + cc) * HD, HD)],
                    w_sem.at[hop, cc, third],
                )
                copy.start()
                weight_loads.setdefault(hop, []).append(copy)
    wo_load = pltpu.make_async_copy(wout_hbm.at[0], wo_ref, wo_sem)
    wo_load.start()

    for copy in loads:
        copy.wait()
    pl.semaphore_wait(barrier, ranks - 1 + 6)

    def cross_copy(index):
        if index < 2:
            lines = pl.ds(index * half, half)
            source, target = xin_ref.at[0, lines], xother_ref.at[0, lines]
        else:
            source, target = xin_ref.at[1], xother_ref.at[1]
        return pltpu.make_async_remote_copy(
            source,
            target,
            cross_send.at[index],
            cross_recv.at[index],
            device_id=(section, other),
            device_id_type=MESH,
        )

    cross_copy(0).start()
    cross_copy(1).start()

    @pl.when(section == 0)
    def _():
        cross_copy(2).start()

    kind_row = jnp.full((1, width), kind_ref[0], jnp.int32)

    def mod_row(index, column):
        text = (column >= text_start // rows).astype(jnp.int32)
        pick = (kind_row == 0) & (jnp.full((1, width), text, jnp.int32) == 1)
        return jnp.where(pick, mod_ref[0, index + 3 : index + 4], mod_ref[0, index : index + 1])

    def mix(x, start, column):
        x = x.astype(jnp.float32)
        center = x - jnp.mean(x, axis=-1, keepdims=True)
        normed = center * lax.rsqrt(jnp.mean(center * center, axis=-1, keepdims=True) + EPS)
        mixed = normed * (1.0 + mod_row(1, column)) + mod_row(0, column)
        mixed_ref[start : start + x.shape[0]] = mixed.astype(jnp.bfloat16)

    chunks = (
        (0, slice(None), 0),
        (0, 0, 1),
        (0, 1, 1),
        (1, 0, slice(None)),
        (1, 1, slice(None)),
    )

    def pieces(chunk):
        return 1 if chunk in (1, 2) else 2

    def cut(ref, chunk):
        return ref.at[0] if pieces(chunk) == 1 else ref

    def exchange(chunk, hop, cc, keys):
        step, halves, column = chunks[chunk]
        target = ((z + hop) % 4) * 4 + xh * 2 + (core + cc) % 2
        if keys:
            source = cut(kvs_ref.at[chunk, hop, cc], chunk)
            there = kv_ref.at[step, place, halves, column]
            sems = kv_send, kv_recv
        else:
            source = cut(qs_ref.at[chunk, hop, cc], chunk)
            there = q_ref.at[step, halves, place, column]
            sems = q_send, q_recv
        return pltpu.make_async_remote_copy(
            source,
            there,
            sems[0].at[chunk, hop, cc],
            sems[1].at[chunk, hop, cc],
            device_id=(section, target),
            device_id_type=MESH,
        )

    def rms(values, gain):
        return (
            values
            * lax.rsqrt(jnp.mean(values * values, axis=-1, keepdims=True) + EPS)
            * gain
        ).astype(jnp.bfloat16)

    def project(chunk):
        step, halves, column = chunks[chunk]
        count = pieces(chunk)
        shape = (count, half, HD) if count == 2 else (half, HD)
        for hop in HOPS:
            if chunk == 0:
                for copy in weight_loads[hop]:
                    copy.wait()
            product = jnp.dot(
                mixed_ref[0 : count * half], w_ref[hop], preferred_element_type=jnp.float32
            )
            for cc in range(2):
                query, key, value = (
                    product[:, (third * 2 + cc) * HD : (third * 2 + cc + 1) * HD]
                    for third in range(3)
                )
                query = rms(query, qg_ref[...]).reshape(shape)
                key = rms(key, kg_ref[...]).reshape(shape)
                value = value.astype(jnp.bfloat16).reshape(shape)
                if hop == 0 and cc == 0:
                    kv_ref[step, place, halves, column, :, 0:HD] = key
                    kv_ref[step, place, halves, column, :, HD : 2 * HD] = value
                    q_ref[step, halves, place, column] = query
                else:
                    first = slice(None) if count == 2 else 0
                    kvs_ref[chunk, hop, cc, first, :, 0:HD] = key
                    kvs_ref[chunk, hop, cc, first, :, HD : 2 * HD] = value
                    qs_ref[chunk, hop, cc, first] = query
                    exchange(chunk, hop, cc, True).start()

    pairs = [(hop, cc) for hop in (0, 3, 2, 1) for cc in range(2) if hop or cc]

    def send_queries(chunk):
        for hop, cc in pairs:
            exchange(chunk, hop, cc, False).start()

    def att_copy(step, n, column, cc):
        step_z = (n + n // 4) % 4
        at = n // 4
        ct = (core + cc) % 2
        return pltpu.make_async_remote_copy(
            atts_ref.at[step, n, ct, column],
            att_ref.at[
                step,
                pl.ds(pl.multiple_of(at * half, half), half),
                pl.ds(pl.multiple_of(rank * HD, HD), HD),
            ],
            att_send.at[step, at, step_z, column, cc],
            att_recv.at[step, at, step_z, column, cc],
            device_id=(
                section,
                ((z + step_z) % 4) * 4 + ((xh + column) % 2) * 2 + ct,
            ),
            device_id_type=MESH,
        )

    def finish(step, at):
        for n in range(4 * at, 4 * at + 4):
            for column in range(2):
                for cc in range(2):
                    if (n + n // 4) % 4 or column or cc:
                        att_copy(step, n, column, cc).wait_recv()
        gate = mod_row(2, rank)
        lines = slice(at * half, (at + 1) * half)
        tile = 512
        for n in range(width // tile):
            cols = slice(n * tile, (n + 1) * tile)
            update = jnp.dot(
                att_ref[step, lines], wo_ref[:, cols], preferred_element_type=jnp.float32
            )
            xsend_ref[step, lines, cols] = (
                xin_ref[step, lines, cols].astype(jnp.float32) + gate[:, cols] * update
            ).astype(jnp.bfloat16)
        for index in range(at * PARTS // 2, (at + 1) * PARTS // 2):
            if step == 1:
                pipe_copy(1, index).start()
            else:

                @pl.when(odd)
                def _():
                    relay_copy(index).start()

                @pl.when(jnp.logical_not(odd))
                def _():
                    pipe_copy(0, index).start()
                    side_copy(index).start()

    def part_of(index):
        return pl.ds(index * part, part)

    def pipe_copy(step, index):
        return pltpu.make_async_remote_copy(
            xsend_ref.at[step, part_of(index)],
            out_ref.at[step, part_of(index)],
            pipe_send.at[step, index],
            pipe_recv.at[step, index],
            device_id=(following, rank),
            device_id_type=MESH,
        )

    def side_copy(index):
        return pltpu.make_async_remote_copy(
            xsend_ref.at[0, part_of(index)],
            xother_ref.at[1, part_of(index)],
            pipe_send.at[2, index],
            pipe_recv.at[2, index],
            device_id=(following, other),
            device_id_type=MESH,
        )

    def relay_copy(index):
        return pltpu.make_async_remote_copy(
            xsend_ref.at[0, part_of(index)],
            relay_ref.at[part_of(index)],
            pipe_send.at[0, index],
            relay_recv.at[index],
            device_id=(ahead, rank),
            device_id_type=MESH,
        )

    def forward_copy(index, which):
        return pltpu.make_async_remote_copy(
            relay_ref.at[part_of(index)],
            (out_ref.at[0] if which == 0 else xother_ref.at[1]).at[part_of(index)],
            relay_send.at[which, index],
            pipe_recv.at[2 * which, index],
            device_id=(before, rank if which == 0 else other),
            device_id_type=MESH,
        )

    def attend(step, live):
        for chunk in range(5):
            if chunks[chunk][0] == step:
                for hop, cc in pairs:
                    exchange(chunk, hop, cc, True).wait_recv()
        spot = lax.broadcasted_iota(jnp.int32, (1, 4 * rows), 1)
        column = (xh + (spot // half) % 2) % 2
        key_rank = 12 + column * 2 + spot // (2 * rows)
        position = key_rank * rows + ((spot // rows) % 2) * half + spot % half
        limit = jnp.full((1, 4 * rows), text_start + live, jnp.int32)
        bias = jnp.where(position < limit, 0.0, -1e30).astype(jnp.float32)
        clear = (ranks - 4) * rows

        def pair(i, carry):
            @pl.when(i == 3)
            def _():
                if step == 0:
                    wo_load.wait()
                finish(step, 0)

            scores = []
            for u in range(2):
                n = 2 * i + u
                at = n // 4
                step_z = (n + at) % 4
                hop = (4 - step_z) % 4
                for cc in range(2):
                    for chunk in range(5):
                        if chunks[chunk][0] == step:
                            if step == 0:
                                due = at == 0
                            else:
                                due = at == chunk - 3
                            if cc == 0:
                                due = due & (step_z > 0)

                            @pl.when(due)
                            def _():
                                exchange(chunk, hop, cc, False).wait_recv()

                zt = (z + step_z) % 4
                query = q_ref[step, at, pl.ds(2 * zt, 2)].reshape(2 * rows, HD)
                keys = kv_ref[step, :, :, :, :, 0:HD].reshape(ranks * rows, HD)
                scores.append(
                    lax.dot_general(
                        query,
                        keys,
                        (((1,), (1,)), ((), ())),
                        preferred_element_type=jnp.float32,
                    )
                )
            for u in range(2):
                n = 2 * i + u
                at = n // 4
                step_z = (n + at) % 4
                score = jnp.concatenate(
                    [scores[u][:, :clear], scores[u][:, clear:] + bias], axis=1
                )
                top = jnp.max(score, axis=-1, keepdims=True)
                weights = jnp.exp2((score - top) * (HD ** (-0.5) * LOG2E))
                denom = jnp.sum(weights, axis=-1, keepdims=True)
                values = kv_ref[step, :, :, :, :, HD : 2 * HD].reshape(ranks * rows, HD)
                summed = jnp.dot(
                    weights.astype(jnp.bfloat16), values, preferred_element_type=jnp.float32
                )
                atts_ref[step, n] = (
                    (summed / denom).astype(jnp.bfloat16).reshape(2, 2, half, HD)
                )

                @pl.when(step_z > 0)
                def _():
                    att_copy(step, n, 0, 0).start()

                @pl.when(step_z == 0)
                def _():
                    att_ref[
                        step,
                        pl.ds(pl.multiple_of(at * half, half), half),
                        pl.ds(pl.multiple_of(rank * HD, HD), HD),
                    ] = atts_ref[step, n, core, 0]

                att_copy(step, n, 0, 1).start()
                att_copy(step, n, 1, 0).start()
                att_copy(step, n, 1, 1).start()
            return carry

        lax.fori_loop(0, 4, pair, 0)
        finish(step, 1)

    mix(xin_ref[0], 0, rank)
    project(0)
    send_queries(0)
    for at in range(2):
        cross_copy(at).wait_recv()
        mix(xother_ref[0, at * half : (at + 1) * half], 0, other)
        project(1 + at)
    send_queries(1)
    send_queries(2)
    attend(0, counts_ref[section])

    @pl.when(odd)
    def _():
        for index in range(PARTS):
            relay_copy(index).wait_recv()
            forward_copy(index, 0).start()

            @pl.when(section != 1)
            def _():
                forward_copy(index, 1).start()

    for at in range(2):
        lines = slice(at * half, (at + 1) * half)
        for index in range(at * PARTS // 2, (at + 1) * PARTS // 2):
            pipe_copy(0, index).wait_recv()

        @pl.when(section > 0)
        def _():
            xin_ref[1, lines] = out_ref[0, lines]
            for index in range(at * PARTS // 2, (at + 1) * PARTS // 2):
                side_copy(index).wait_recv()

        if at == 0:

            @pl.when(section == 0)
            def _():
                cross_copy(2).wait_recv()

        mix(xin_ref[1, lines], 0, rank)
        mix(xother_ref[1, lines], half, other)
        project(3 + at)
    send_queries(3)
    send_queries(4)
    attend(1, counts_ref[(section + sections) % (sections + 1)])

    cross_copy(0).wait_send()
    cross_copy(1).wait_send()

    @pl.when(section == 0)
    def _():
        cross_copy(2).wait_send()

    @pl.when(jnp.logical_not(odd))
    def _():
        for index in range(PARTS):
            side_copy(index).wait_send()

    @pl.when(odd)
    def _():
        for index in range(PARTS):
            forward_copy(index, 0).wait_send()

            @pl.when(section != 1)
            def _():
                forward_copy(index, 1).wait_send()

    for index in range(PARTS):
        pipe_copy(0, index).wait_send()
    for chunk in range(5):
        for hop, cc in pairs:
            exchange(chunk, hop, cc, True).wait_send()
            exchange(chunk, hop, cc, False).wait_send()
    for step in range(2):
        for n in range(8):
            for column in range(2):
                for cc in range(2):
                    if (n + n // 4) % 4 or column or cc:
                        att_copy(step, n, column, cc).wait_send()
    for index in range(PARTS):
        pipe_copy(1, index).wait()


def shards(held, entering, counts, kind, modulation, w_qkv, w_out, q_gain, k_gain):
    rows, width = entering.shape
    half = rows // 2
    inner = w_out.shape[1]
    bf16 = jnp.bfloat16
    vmem = pl.BlockSpec(memory_space=pltpu.VMEM)
    smem = pl.BlockSpec(memory_space=pltpu.SMEM)
    hbm = pl.BlockSpec(memory_space=pl.ANY)
    dma = pltpu.SemaphoreType.DMA
    out = pl.pallas_call(
        body,
        out_shape=jax.ShapeDtypeStruct((2, rows, width), bf16),
        in_specs=[smem, smem, hbm, hbm, vmem, hbm, hbm, vmem, vmem],
        out_specs=vmem,
        scratch_shapes=[
            pltpu.VMEM((4, width, 6 * HD), bf16),
            pltpu.VMEM((inner, width), bf16),
            pltpu.VMEM((2, rows, width), bf16),
            pltpu.VMEM((2, rows, width), bf16),
            pltpu.VMEM((2, rows, width), bf16),
            pltpu.VMEM((rows, width), bf16),
            pltpu.VMEM((rows, width), bf16),
            pltpu.VMEM((2, 8, 2, 2, half, 2 * HD), bf16),
            pltpu.VMEM((2, 2, 8, 2, half, HD), bf16),
            pltpu.VMEM((5, 4, 2, 2, half, 2 * HD), bf16),
            pltpu.VMEM((5, 4, 2, 2, half, HD), bf16),
            pltpu.VMEM((2, rows, inner), bf16),
            pltpu.VMEM((2, 8, 2, 2, half, HD), bf16),
            dma((2,)),
            dma((4, 2, 3)),
            dma,
            dma((3,)),
            dma((3,)),
            dma((5, 4, 2)),
            dma((5, 4, 2)),
            dma((5, 4, 2)),
            dma((5, 4, 2)),
            dma((2, 2, 4, 2, 2)),
            dma((2, 2, 4, 2, 2)),
            dma((3, PARTS)),
            dma((3, PARTS)),
            dma((PARTS,)),
            dma((2, PARTS)),
        ],
        compiler_params=pltpu.CompilerParams(
            collective_id=0, has_side_effects=True, vmem_limit_bytes=60 * 1024 * 1024
        ),
        name="relay",
    )(counts, kind, held, entering, modulation, w_qkv, w_out, q_gain, k_gain)
    return out[:, None]


def solution(mesh):
    placed = (
        P("pipe", "seq", None),
        P("seq", None),
        P(),
        P("pipe"),
        P("pipe", None, None),
        P("pipe", None, None),
        P("pipe", None, None),
        P("pipe", None),
        P("pipe", None),
    )
    return jax.shard_map(
        shards, mesh=mesh, in_specs=placed, out_specs=P(None, "pipe", "seq", None), check_vma=False
    )
```

time: 110 us -> 103 us (0.936)
  the two profiles are of different devices: /device:TPU:26 before, /device:TPU:1 now
where the time goes in v2:
time: 103 us; the launch traced here: 102 us
  Pallas kernels  98.4 us (96%)
  local copies, waits for them, and re-layouts  3.46 us (3%)
    pallas_call x1, Pallas kernels, shards(): pl.pallas_call(body, out_shape=jax.ShapeDtypeStruct((2, rows, width), bf1...  98.4 us
    unnamed x2, local copies, waits for them, and re-layouts  3.46 us

profile of v2, /device:TPU:1, one launch (start us, length us, event | category | flops | bytes accessed | tf_op | source)
XLA Modules:
  0.0 102.5 jit_solution(6765715260794919388)
XLA Ops:
  0.7 1.4 %copy.10.mod_ref = f32[1,6,1536]{2,1,0:T(8,128)} copy(f32[1,6,1536]{2,0,1:T(1,128)} %param.13) | data formatting | bytes 73728 | tf_op args[4]
  2.0 98.4 %relay.1 = bf16[2,128,1536]{2,1,0:T(8,128)(2,1)} custom-call(s32[9]{0:T(128)} %counts_ref.1, s32[1]{0:T(128)S(6)} %copy.13.kind_ref, bf16[1,128,1536]{2,1,0:T(8,128)(2,1)} %held_hbm.1, bf16[128,1536]{1,0:T(8,128)(2,1)} %entering_hbm.1, f32[1,6,1536]{2,1,0:T(8,128)} %copy.10.mod_ref, bf16[1,1536,6144]{2,1,0:T(8,128)(2,1)} %wqkv_hbm.1, ...), custom_call_target="tpu_custom_call" | custom-call | tf_op jit(solution)/shard_map/relay/pallas_call | solution.py:503
  100.4 2.1 %copy.14 = bf16[2,1,128,1536]{3,2,1,0:T(8,128)(2,1)} copy(bf16[2,1,128,1536]{3,2,1,0:T(8,128)(2,1)} %bitcast.3) | data formatting | bytes 1572864

commit v3 on v2

--- a/solution.py
+++ b/solution.py
@@ -104,10 +104,16 @@
                     w_ref.at[hop, :, pl.ds((third * 2 + cc) * HD, HD)],
                     w_sem.at[hop, cc, third],
                 )
-                copy.start()
                 weight_loads.setdefault(hop, []).append(copy)
     wo_load = pltpu.make_async_copy(wout_hbm.at[0], wo_ref, wo_sem)
-    wo_load.start()
+
+    def start_weights(index):
+        if index < len(HOPS):
+            for copy in weight_loads[HOPS[index]]:
+                copy.start()
+
+    start_weights(0)
+    start_weights(1)
 
     for copy in loads:
         copy.wait()
@@ -140,7 +146,7 @@
     def mod_row(index, column):
         text = (column >= text_start // rows).astype(jnp.int32)
         pick = (kind_row == 0) & (jnp.full((1, width), text, jnp.int32) == 1)
-        return jnp.where(pick, mod_ref[0, index + 3 : index + 4], mod_ref[0, index : index + 1])
+        return jnp.where(pick, mod_ref[index + 3], mod_ref[index])
 
     def mix(x, start, column):
         x = x.astype(jnp.float32)
@@ -194,10 +200,11 @@
         step, halves, column = chunks[chunk]
         count = pieces(chunk)
         shape = (count, half, HD) if count == 2 else (half, HD)
-        for hop in HOPS:
+        for index, hop in enumerate(HOPS):
             if chunk == 0:
                 for copy in weight_loads[hop]:
                     copy.wait()
+                start_weights(index + 2)
             product = jnp.dot(
                 mixed_ref[0 : count * half], w_ref[hop], preferred_element_type=jnp.float32
             )
@@ -412,6 +419,7 @@
     mix(xin_ref[0], 0, rank)
     project(0)
     send_queries(0)
+    wo_load.start()
     for at in range(2):
         cross_copy(at).wait_recv()
         mix(xother_ref[0, at * half : (at + 1) * half], 0, other)
@@ -539,7 +547,7 @@
             collective_id=0, has_side_effects=True, vmem_limit_bytes=60 * 1024 * 1024
         ),
         name="relay",
-    )(counts, kind, held, entering, modulation, w_qkv, w_out, q_gain, k_gain)
+    )(counts, kind, held, entering, modulation.transpose(1, 0, 2), w_qkv, w_out, q_gain, k_gain)
     return out[:, None]
 
 

time: 103 us -> 100 us (0.971)
  Pallas kernels: 98.4 us -> 97 us
  local copies, waits for them, and re-layouts: 3.46 us -> 2.06 us
    unnamed x2 -> x1, local copies, waits for them, and re-layouts: 3.46 us -> 2.06 us
    pallas_call x1, Pallas kernels: 98.4 us -> 97 us  [shards(): pl.pallas_call(body, out_shape=jax.ShapeDtypeStruct((2, rows, width), bf1...]
where the time goes in v3:
time: 100 us; the launch traced here: 99.7 us
  Pallas kernels  97 us (97%)
  local copies, waits for them, and re-layouts  2.06 us (2%)
    pallas_call x1, Pallas kernels, shards(): pl.pallas_call(body, out_shape=jax.ShapeDtypeStruct((2, rows, width), bf1...  97 us
    unnamed x1, local copies, waits for them, and re-layouts  2.06 us

profile of v3, /device:TPU:1, one launch (start us, length us, event | category | flops | bytes accessed | tf_op | source)
XLA Modules:
  0.0 99.7 jit_solution(4126869036010459573)
XLA Ops:
  0.7 97.0 %relay.1 = bf16[2,128,1536]{2,1,0:T(8,128)(2,1)} custom-call(s32[9]{0:T(128)} %counts_ref.1, s32[1]{0:T(128)S(6)} %copy.12.kind_ref, bf16[1,128,1536]{2,1,0:T(8,128)(2,1)} %held_hbm.1, bf16[128,1536]{1,0:T(8,128)(2,1)} %entering_hbm.1, f32[6,1,1536]{2,1,0:T(1,128)} %bitcast.5, bf16[1,1536,6144]{2,1,0:T(8,128)(2,1)} %wqkv_hbm.1, ...), custom_call_target="tpu_custom_call" | custom-call | tf_op jit(solution)/shard_map/relay/pallas_call | solution.py:511
  97.6 2.1 %copy.13 = bf16[2,1,128,1536]{3,2,1,0:T(8,128)(2,1)} copy(bf16[2,1,128,1536]{3,2,1,0:T(8,128)(2,1)} %bitcast.4) | data formatting | bytes 1572864

commit v4 on v3

--- a/solution.py
+++ b/solution.py
@@ -259,6 +259,8 @@
                 for cc in range(2):
                     if (n + n // 4) % 4 or column or cc:
                         att_copy(step, n, column, cc).wait_recv()
+        if step == 0 and at == 1:
+            forward(0, 1)
         gate = mod_row(2, rank)
         lines = slice(at * half, (at + 1) * half)
         tile = 512
@@ -327,6 +329,17 @@
             device_id_type=MESH,
         )
 
+    def forward(first, last):
+        @pl.when(odd)
+        def _():
+            for index in range(first, last):
+                relay_copy(index).wait_recv()
+                forward_copy(index, 0).start()
+
+                @pl.when(section != 1)
+                def _():
+                    forward_copy(index, 1).start()
+
     def attend(step, live):
         for chunk in range(5):
             if chunks[chunk][0] == step:
@@ -341,7 +354,7 @@
         clear = (ranks - 4) * rows
 
         def pair(i, carry):
-            @pl.when(i == 3)
+            @pl.when(i == 2 + step)
             def _():
                 if step == 0:
                     wo_load.wait()
@@ -428,18 +441,9 @@
     send_queries(2)
     attend(0, counts_ref[section])
 
-    @pl.when(odd)
-    def _():
-        for index in range(PARTS):
-            relay_copy(index).wait_recv()
-            forward_copy(index, 0).start()
-
-            @pl.when(section != 1)
-            def _():
-                forward_copy(index, 1).start()
-
     for at in range(2):
         lines = slice(at * half, (at + 1) * half)
+        forward(max(1, at * PARTS // 2), (at + 1) * PARTS // 2)
         for index in range(at * PARTS // 2, (at + 1) * PARTS // 2):
             pipe_copy(0, index).wait_recv()
 

time: 100 us -> 100 us (level)
  no operation moved by 1% of the time
where the time goes in v4:
time: 100 us; the launch traced here: 99.6 us
  Pallas kernels  96.9 us (97%)
  local copies, waits for them, and re-layouts  2.06 us (2%)
    pallas_call x1, Pallas kernels, shards(): pl.pallas_call(body, out_shape=jax.ShapeDtypeStruct((2, rows, width), bf1...  96.9 us
    unnamed x1, local copies, waits for them, and re-layouts  2.06 us

profile of v4, /device:TPU:1, one launch (start us, length us, event | category | flops | bytes accessed | tf_op | source)
XLA Modules:
  0.0 99.6 jit_solution(12560993240827265037)
XLA Ops:
  0.7 96.9 %relay.1 = bf16[2,128,1536]{2,1,0:T(8,128)(2,1)} custom-call(s32[9]{0:T(128)} %counts_ref.1, s32[1]{0:T(128)S(6)} %copy.12.kind_ref, bf16[1,128,1536]{2,1,0:T(8,128)(2,1)} %held_hbm.1, bf16[128,1536]{1,0:T(8,128)(2,1)} %entering_hbm.1, f32[6,1,1536]{2,1,0:T(1,128)} %bitcast.5, bf16[1,1536,6144]{2,1,0:T(8,128)(2,1)} %wqkv_hbm.1, ...), custom_call_target="tpu_custom_call" | custom-call | tf_op jit(solution)/shard_map/relay/pallas_call | solution.py:515
  97.5 2.1 %copy.13 = bf16[2,1,128,1536]{3,2,1,0:T(8,128)(2,1)} copy(bf16[2,1,128,1536]{3,2,1,0:T(8,128)(2,1)} %bitcast.4) | data formatting | bytes 1572864
